TPU v7x, 32 devices: a whole 2x2x4 slice. The times are simulated.
32 devices in a mesh: groups: 2 (over y), frames: 16 (over z, x, core).
Axes of the slice: x: 2, y: 2, z: 4, core: 2. Of those that a mesh axis runs over, the one named last changes fastest.
Arguments:
- video_frames: bfloat16 [64, 1024, 1024], P(('groups', 'frames')), parts along dimension 0, may hold values from -6 to 6
- segments: int32 [64], P('groups'), parts along dimension 0, may hold values from 0 to 3, never falling along the last dimension, each value on 1 to 29 neighbouring positions
- ref_pick: int32 [8], P('groups'), parts along dimension 0, may hold values from 0 to 4095
- band_taps: bfloat16 [32], replicated, may hold values from -2 to 2
Outputs:
- motion: float32 [64, 256, 256], P(('groups', 'frames')), parts along dimension 0
There are 2 independent parts, one for each index of `groups`. A program takes and returns all parts, laid end to end along the dimension named above; an argument that names none is the same for every part. Nothing has to cross between parts.
Inputs may be any that keep to these rules, and one draw needn't show every extreme that they name: Segment numbers never fall along the frames; each of the 4 segments holds 1 to 29 frames and one holds exactly 29.
All inputs are finite; a program needn't handle non-finite values.
Results may differ from a plain program's by a relative error of at most 0.012.
Values may be sent and summed in bfloat16 or wider, within the bound.
A program may use at most 128 MiB of HBM per device.

v0:
```python
import math

import jax
import numpy as np
import jax.numpy as jnp
from jax import lax
from jax.experimental import pallas as pl
from jax.experimental.pallas import tpu as pltpu
from jax.sharding import PartitionSpec as P

IMG = 1024
ORIENT = 4
NSEG = 4
QUART = 256


blur_sigma = 2.0
gabor_sigma = 2.0
wave_number = math.pi / 2.0
gabor_gain = 2.0


def spread(x, axis, root):
    mine = lax.axis_index(axis) == root
    return lax.psum(jnp.where(mine, x, jnp.zeros_like(x)), axis)


def make_down(full_size, quarter):
    position = jnp.arange(quarter, dtype=jnp.float32)[:, None]
    columns = jnp.arange(full_size, dtype=jnp.float32)[None, :]
    offset_grid = columns - 4.0 * position - 1.5
    weight = jnp.exp(-offset_grid * offset_grid / (2.0 * blur_sigma * blur_sigma))
    return (weight / jnp.sum(weight, axis=1, keepdims=True)).astype(jnp.bfloat16)


def gabor_tables(quarter, orient):
    position = jnp.arange(quarter, dtype=jnp.float32)
    offset_grid = position[None, :] - position[:, None]
    envelope = gabor_gain * jnp.exp(-offset_grid * offset_grid / (2.0 * gabor_sigma * gabor_sigma))
    angles = jnp.arange(orient, dtype=jnp.float32) * (math.pi / orient)
    wave_x = wave_number * jnp.cos(angles)
    wave_y = wave_number * jnp.sin(angles)
    phase_y = wave_y[:, None, None] * offset_grid[None]
    left_table = jnp.stack([envelope * jnp.cos(phase_y), envelope * jnp.sin(phase_y)], axis=2)
    left_table = left_table.reshape(orient * quarter * 2, quarter).astype(jnp.bfloat16)
    phase_x = wave_x[:, None, None] * (-offset_grid)[None]
    real_part = envelope * jnp.cos(phase_x)
    imag_part = envelope * jnp.sin(phase_x)
    upper_half = jnp.concatenate([real_part, imag_part], axis=2)
    lower_half = jnp.concatenate([-imag_part, real_part], axis=2)
    right_table = jnp.concatenate([upper_half, lower_half], axis=1).astype(jnp.bfloat16)
    return (left_table, right_table)


def phase_terms(coeffs, per_frame):
    quarter = coeffs.shape[-1] // 2
    coeff_real = coeffs[..., :quarter].astype(jnp.float32)
    coeff_imag = coeffs[..., quarter:].astype(jnp.float32)
    ref_real = per_frame[..., :quarter].astype(jnp.float32)
    ref_imag = per_frame[..., quarter:].astype(jnp.float32)
    prod_real = coeff_real * ref_real + coeff_imag * ref_imag
    prod_imag = coeff_imag * ref_real - coeff_real * ref_imag
    phase_signal = (
        prod_imag / jnp.sqrt(prod_real * prod_real + prod_imag * prod_imag + 1.0)
    ).astype(jnp.bfloat16)
    amplitude = coeff_real * coeff_real + coeff_imag * coeff_imag
    return (phase_signal, amplitude)


def taps_matrix(band_taps, frame_count):
    frame_index = jnp.arange(frame_count, dtype=jnp.int32)
    lag_grid = frame_index[:, None] - frame_index[None, :]
    one_hot = (
        lag_grid[:, :, None] == jnp.arange(band_taps.shape[0], dtype=jnp.int32)[None, None, :]
    ).astype(jnp.float32)
    return jnp.einsum("tsk,k->ts", one_hot, band_taps.astype(jnp.float32)).astype(jnp.bfloat16)


def segment_refs(segments, ref_pick, segment_count):
    numbers = jnp.arange(segment_count, dtype=jnp.int32)
    starts = jnp.sum((segments[None, :] < numbers[:, None]).astype(jnp.int32), axis=1)
    counts = jnp.sum((segments[None, :] == numbers[:, None]).astype(jnp.int32), axis=1)
    return starts + ref_pick % counts


def body(video_frames, segments, ref_pick, band_taps):
    frames_here = video_frames.shape[0]
    down_matrix = make_down(IMG, QUART)
    left_table, right_table = gabor_tables(QUART, ORIENT)

    def reduce_frames(pictures):
        half_done = jnp.einsum(
            "nia,qa->niq", pictures, down_matrix, preferred_element_type=jnp.float32
        ).astype(jnp.bfloat16)
        return jnp.einsum(
            "qi,nik->nqk", down_matrix, half_done, preferred_element_type=jnp.float32
        ).astype(jnp.bfloat16)

    def filter_frames(reduced):
        stacked = jnp.einsum(
            "ra,nak->nrk", left_table, reduced, preferred_element_type=jnp.float32
        ).astype(jnp.bfloat16)
        stacked = stacked.reshape(reduced.shape[0], ORIENT, QUART, 2 * QUART)
        return jnp.einsum(
            "noya,oab->noyb", stacked, right_table, preferred_element_type=jnp.float32
        ).astype(jnp.bfloat16)

    small_own = reduce_frames(video_frames)
    coeff_own = filter_frames(small_own)
    ref_frames = segment_refs(segments, ref_pick, NSEG)
    gathered = []
    for segment in range(NSEG):
        root_index = ref_frames[segment] // frames_here
        local_index = ref_frames[segment] % frames_here
        payload = lax.dynamic_index_in_dim(video_frames, local_index, 0, keepdims=False)
        gathered.append(spread(payload, "frames", root_index))
    ref_coeff = filter_frames(reduce_frames(jnp.stack(gathered)))
    first_frame = lax.axis_index("frames") * frames_here
    own_ids = lax.dynamic_slice_in_dim(segments, first_frame, frames_here)
    select = (own_ids[:, None] == jnp.arange(NSEG, dtype=jnp.int32)[None, :]).astype(jnp.bfloat16)
    per_frame = jnp.dot(select, ref_coeff.reshape(NSEG, -1), preferred_element_type=jnp.float32)
    per_frame = per_frame.astype(jnp.bfloat16).reshape(coeff_own.shape)
    phase_signal, amplitude = phase_terms(coeff_own, per_frame)
    phase_signal = phase_signal.reshape(frames_here, ORIENT, QUART * QUART)
    pixel_rows = lax.all_to_all(phase_signal, "frames", split_axis=2, concat_axis=0, tiled=True)
    matrix = taps_matrix(band_taps, pixel_rows.shape[0])
    filtered = jnp.einsum(
        "ts,sop->top", matrix, pixel_rows, preferred_element_type=jnp.float32
    ).astype(jnp.bfloat16)
    filtered = lax.all_to_all(filtered, "frames", split_axis=0, concat_axis=2, tiled=True)
    filtered = filtered.reshape(frames_here, ORIENT, QUART, QUART).astype(jnp.float32)
    return jnp.sum(amplitude * filtered, axis=1) / (jnp.sum(amplitude, axis=1) + 1.0)


PICK_LIMIT = 4096
REACH = 32


def down_table():
    position = np.arange(QUART, dtype=np.float32)[:, None]
    columns = np.arange(IMG, dtype=np.float32)[None, :]
    offset = columns - np.float32(4.0) * position - np.float32(1.5)
    weight = np.exp(-offset * offset / np.float32(2.0 * blur_sigma * blur_sigma))
    return (weight / np.sum(weight, axis=1, keepdims=True)).astype(jnp.bfloat16)


def waves():
    angles = np.arange(ORIENT, dtype=np.float32) * np.float32(math.pi / ORIENT)
    return np.float32(wave_number) * np.cos(angles), np.float32(wave_number) * np.sin(angles)


def gabor_envelope(offset):
    return np.float32(gabor_gain) * np.exp(-offset * offset / np.float32(2.0 * gabor_sigma * gabor_sigma))


def left_window(rows):
    offset = (
        np.arange(rows + 2 * REACH, dtype=np.float32)[None, :]
        - REACH
        - np.arange(rows, dtype=np.float32)[:, None]
    )
    envelope = gabor_envelope(offset)
    phase = waves()[1][:, None, None] * offset[None]
    table = np.stack([envelope * np.cos(phase), envelope * np.sin(phase)], axis=1)
    return table.reshape(ORIENT * 2 * rows, -1).astype(jnp.bfloat16)


def right_tables():
    position = np.arange(QUART, dtype=np.float32)
    offset = position[:, None] - position[None, :]
    envelope = gabor_envelope(offset)
    phase = waves()[0][:, None, None] * offset[None]
    real, imag = envelope * np.cos(phase), envelope * np.sin(phase)
    upper = np.concatenate([real, imag], axis=2)
    lower = np.concatenate([-imag, real], axis=2)
    return np.stack([upper, lower], axis=1).astype(jnp.bfloat16)


PLANE = 4
PAIR = 2


def flip(number, bits):
    step = 1
    while step <= bits:
        if bits & step:
            number = number + step - 2 * step * ((number // step) % 2)
        step *= 2
    return number


def make_kernel(parts, here, rows):
    frames = parts * here
    planes = parts // PLANE
    window = rows + 2 * REACH
    pair_window = PAIR * rows + 2 * REACH
    plane_window = PLANE * rows + 2 * REACH
    total = frames * rows
    chunks = 2

    def kernel(
        segments, picks, taps, video_hbm, down_hbm, down_t_hbm, left, right_hbm, out_hbm,
        video, down, down_t, right, half, reduced, gathered, stacked, coeffs,
        phase, matrix, numer, denom, moved,
        load_sem, store_sem, send_1, recv_1, send_2, recv_2, send_3, recv_3, send_b, recv_b,
    ):
        me = lax.axis_index("frames")
        plane, spot = me // PLANE, me % PLANE
        across, sibling = flip(spot, PAIR), flip(spot, 1)
        barrier = pltpu.get_barrier_semaphore()

        def peer(j):
            return lax.rem(me + j, parts)

        def piece(n, part):
            height = IMG // chunks
            where = pl.ds(part * height, height)
            return pltpu.make_async_copy(
                video_hbm.at[n, where], video.at[n, where], load_sem.at[3 + n * chunks + part]
            )

        load_down_t = pltpu.make_async_copy(down_t_hbm, down_t, load_sem.at[0])
        load_down = pltpu.make_async_copy(down_hbm, down, load_sem.at[1])
        load_right = pltpu.make_async_copy(right_hbm, right, load_sem.at[2])
        load_down_t.start()
        for n in range(here):
            for part in range(chunks):
                piece(n, part).start()
            if n == 0:
                load_down.start()
        load_right.start()

        blank = jnp.zeros((frames, REACH, QUART), jnp.bfloat16)

        @pl.when(plane == 0)
        def _():
            gathered[:, :REACH, :] = blank

        @pl.when(plane == planes - 1)
        def _():
            gathered[:, plane_window - REACH :, :] = blank

        @pl.loop(1, parts)
        def _(j):
            pl.semaphore_signal(barrier, inc=1, device_id={"frames": peer(j)})

        edge = jnp.zeros((here, REACH, QUART), jnp.bfloat16)
        reduced[:, :REACH, :] = edge
        reduced[:, REACH + QUART :, :] = edge

        def frame_of(j, where, n):
            return (flip(plane, j) * PLANE + where) * here + n

        def rows_of(j, n, first, size):
            if j == 0:
                start = pl.multiple_of((plane * PLANE + first) * rows, rows)
                return reduced.at[n, pl.ds(start, size), :]
            return gathered.at[frame_of(j, spot, n), pl.ds(pl.multiple_of(first * rows, rows), size), :]

        def copy_1(j, n, low, high):
            to = flip(plane, j)
            start = pl.multiple_of(to * PLANE * rows + low, rows)
            return pltpu.make_async_remote_copy(
                src_ref=reduced.at[n, pl.ds(start, high - low), :],
                dst_ref=gathered.at[me * here + n, pl.ds(low, high - low), :],
                send_sem=send_1.at[j, n],
                recv_sem=recv_1.at[j, n],
                device_id={"frames": to * PLANE + spot},
            )

        def each_1(j, n, to, act):
            @pl.when(to == 0)
            def _():
                act(copy_1(j, n, REACH, plane_window))

            @pl.when(to == planes - 1)
            def _():
                act(copy_1(j, n, 0, plane_window - REACH))

            if planes > 2:

                @pl.when((to > 0) & (to < planes - 1))
                def _():
                    act(copy_1(j, n, 0, plane_window))

        def copy_2(j, n):
            first = across // PAIR * PAIR
            where = pl.ds(pl.multiple_of(first * rows, rows), pair_window)
            return pltpu.make_async_remote_copy(
                src_ref=rows_of(j, n, first, pair_window),
                dst_ref=gathered.at[frame_of(j, spot, n), where, :],
                send_sem=send_2.at[j, n],
                recv_sem=recv_2.at[j, n],
                device_id={"frames": plane * PLANE + across},
            )

        sibling_rows = pl.ds(pl.multiple_of(sibling * rows, rows), window)

        def copy_3(j, n):
            return pltpu.make_async_remote_copy(
                src_ref=rows_of(j, n, sibling, window),
                dst_ref=gathered.at[frame_of(j, spot, n), sibling_rows, :],
                send_sem=send_3.at[j, n],
                recv_sem=recv_3.at[j, n],
                device_id={"frames": plane * PLANE + sibling},
            )

        def copy_4(j, n):
            part = gathered.at[frame_of(j, across, n), sibling_rows, :]
            return pltpu.make_async_remote_copy(
                src_ref=part,
                dst_ref=part,
                send_sem=send_3.at[planes + j, n],
                recv_sem=recv_3.at[planes + j, n],
                device_id={"frames": plane * PLANE + sibling},
            )

        load_down_t.wait()
        for n in range(here):
            for part in range(chunks):
                piece(n, part).wait()
                where = slice(part * (IMG // chunks), (part + 1) * (IMG // chunks))
                half[n, where] = jnp.dot(
                    video[n, where], down_t[...], preferred_element_type=jnp.float32
                ).astype(jnp.bfloat16)
            if n == 0:
                load_down.wait()
            reduced[n, REACH : REACH + QUART, :] = jnp.dot(
                down[...], half[n], preferred_element_type=jnp.float32
            ).astype(jnp.bfloat16)
            if n == 0:
                pl.semaphore_wait(barrier, parts - 1)
            for j in range(1, planes):
                each_1(j, n, flip(plane, j), lambda copy: copy.start())
            copy_2(0, n).start()
            copy_3(0, n).start()

        lag = lax.broadcasted_iota(jnp.int32, (frames, frames), 0) - lax.broadcasted_iota(
            jnp.int32, (frames, frames), 1
        )
        toeplitz = jnp.zeros((frames, frames), jnp.float32)
        tap_row = taps[...].astype(jnp.float32)
        for k in range(min(taps.shape[1], frames)):
            toeplitz = jnp.where(lag == k, tap_row[:, k : k + 1], toeplitz)
        owner = lax.broadcasted_iota(jnp.int32, (total, frames), 0) // rows
        repeat = jnp.where(
            owner == lax.broadcasted_iota(jnp.int32, (total, frames), 1), 1.0, 0.0
        ).astype(jnp.bfloat16)
        tall = jnp.dot(
            repeat, toeplitz.astype(jnp.bfloat16), preferred_element_type=jnp.float32
        ).astype(jnp.bfloat16)
        wide = lax.dot_general(
            tall, repeat, (((1,), (1,)), ((), ())), preferred_element_type=jnp.float32
        )
        same = (
            lax.broadcasted_iota(jnp.int32, (total, total), 0) % rows
            == lax.broadcasted_iota(jnp.int32, (total, total), 1) % rows
        )
        matrix[...] = jnp.where(same, wide, 0.0).astype(jnp.bfloat16)

        def stack_one(place, block):
            stacked[place] = (
                jnp.dot(left[...], block, preferred_element_type=jnp.float32)
                .astype(jnp.bfloat16)
                .reshape(ORIENT * 2, rows, QUART)
            )

        def coefficients(where):
            for o in range(ORIENT):
                value = jnp.dot(
                    stacked[:, where, :, 2 * o].reshape(planes * here * rows, QUART),
                    right[o, 0],
                    preferred_element_type=jnp.float32,
                ) + jnp.dot(
                    stacked[:, where, :, 2 * o + 1].reshape(planes * here * rows, QUART),
                    right[o, 1],
                    preferred_element_type=jnp.float32,
                )
                value = value.astype(jnp.bfloat16).reshape(planes, here, rows, 2 * QUART)
                for p in range(planes):
                    coeffs[pl.ds((p * PLANE + where) * here, here), o] = value[p]

        own_rows = pl.ds(pl.multiple_of(spot * rows, rows), window)

        def stack_arrived(j, where):
            @pl.loop(0, here)
            def _(n):
                t = frame_of(j, where, n)
                stack_one((flip(plane, j), where, n), gathered[t, own_rows, :])

        def second(j):
            for n in range(here):
                copy_2(j, n).wait_recv()
                copy_4(j, n).start()
            stack_arrived(j, across)

        for n in range(here):
            stack_one((plane, spot, n), reduced[n, pl.ds(pl.multiple_of(me * rows, rows), window), :])
        for n in range(here):
            for j in range(1, planes):
                each_1(j, n, plane, lambda copy: copy.wait_recv())
                copy_2(j, n).start()
                copy_3(j, n).start()
        for j in range(1, planes):
            stack_arrived(j, spot)
        load_right.wait()
        for j in range(planes):
            second(j)
        coefficients(spot)
        for j in range(planes):
            for n in range(here):
                copy_3(j, n).wait_recv()
            stack_arrived(j, sibling)
        coefficients(across)
        coefficients(sibling)
        last = flip(across, 1)
        for j in range(planes):
            for n in range(here):
                copy_4(j, n).wait_recv()
            stack_arrived(j, last)
        coefficients(last)

        counts = [jnp.int32(0)] * NSEG
        for t in range(frames):
            for s in range(NSEG):
                counts[s] = counts[s] + jnp.where(segments[t] == s, 1, 0)
        picked, first = [], jnp.int32(0)
        for s in range(NSEG):
            rest = picks[s]
            for bit in reversed(range((PICK_LIMIT - 1).bit_length())):
                rest = jnp.where(rest >= counts[s] * (1 << bit), rest - counts[s] * (1 << bit), rest)
            picked.append(first + rest)
            first = first + counts[s]

        @pl.loop(0, frames)
        def _(t):
            ref = picked[NSEG - 1]
            for s in range(NSEG - 1):
                ref = jnp.where(segments[t] == s, picked[s], ref)
            ones = coeffs[t].astype(jnp.float32)
            base = coeffs[ref].astype(jnp.float32)
            real, imag = ones[..., :QUART], ones[..., QUART:]
            ref_real, ref_imag = base[..., :QUART], base[..., QUART:]
            prod_real = real * ref_real + imag * ref_imag
            prod_imag = imag * ref_real - real * ref_imag
            signal = prod_imag * lax.rsqrt(prod_real * prod_real + prod_imag * prod_imag + 1.0)
            phase[:, t] = signal.astype(jnp.bfloat16)
            denom[t] = jnp.sum(real * real + imag * imag, axis=0) + 1.0

        here_rows = pl.ds(pl.multiple_of(me * rows, rows), rows)

        def return_copy(j):
            to = peer(j)
            return pltpu.make_async_remote_copy(
                src_ref=moved.at[pl.ds(to * here, here)],
                dst_ref=out_hbm.at[:, here_rows, :],
                send_sem=send_b.at[j],
                recv_sem=recv_b.at[j],
                device_id={"frames": to},
            )

        crowd = parts // 2
        near = me // crowd

        def filter_half(number):
            span = pl.ds(number * (frames // 2), frames // 2)
            long_span = pl.ds(pl.multiple_of(number * (total // 2), total // 2), total // 2)
            for o in range(ORIENT):
                filtered = (
                    jnp.dot(
                        matrix[long_span, :],
                        phase[o].reshape(total, QUART),
                        preferred_element_type=jnp.float32,
                    )
                    .astype(jnp.bfloat16)
                    .astype(jnp.float32)
                    .reshape(frames // 2, rows, QUART)
                )
                real = coeffs[span, o, :, :QUART].astype(jnp.float32)
                imag = coeffs[span, o, :, QUART:].astype(jnp.float32)
                term = (real * real + imag * imag) * filtered
                if o == 0:
                    numer[...] = term
                elif o < ORIENT - 1:
                    numer[...] += term
                else:
                    moved[span] = ((numer[...] + term) / denom[span]).astype(jnp.bfloat16)

        filter_half(1 - near)

        @pl.loop(0, crowd)
        def _(k):
            to = (1 - near) * crowd + lax.rem(me + k, crowd)
            return_copy(lax.rem(to + parts - me, parts)).start()

        filter_half(near)

        @pl.loop(1, crowd)
        def _(k):
            to = near * crowd + lax.rem(me + k, crowd)
            return_copy(lax.rem(to + parts - me, parts)).start()

        store = pltpu.make_async_copy(
            moved.at[pl.ds(me * here, here)], out_hbm.at[:, here_rows, :], store_sem
        )
        store.start()

        for n in range(here):
            for j in range(planes):
                if j:
                    each_1(j, n, flip(plane, j), lambda copy: copy.wait_send())
                copy_2(j, n).wait_send()
                copy_3(j, n).wait_send()
                copy_4(j, n).wait_send()

        @pl.loop(1, parts)
        def _(j):
            return_copy(j).wait_recv()

        @pl.loop(1, parts)
        def _(j):
            return_copy(j).wait_send()

        store.wait()

    bf16, f32, dma = jnp.bfloat16, jnp.float32, pltpu.SemaphoreType.DMA
    anywhere = pl.BlockSpec(memory_space=pl.ANY)
    vmem = pl.BlockSpec(memory_space=pltpu.VMEM)
    smem = pl.BlockSpec(memory_space=pltpu.SMEM)
    return pl.pallas_call(
        kernel,
        out_shape=jax.ShapeDtypeStruct((here, QUART, QUART), bf16),
        in_specs=[smem, smem, vmem, anywhere, anywhere, anywhere, vmem, anywhere],
        out_specs=anywhere,
        scratch_shapes=[
            pltpu.VMEM((here, IMG, IMG), bf16),
            pltpu.VMEM((QUART, IMG), bf16),
            pltpu.VMEM((IMG, QUART), bf16),
            pltpu.VMEM((ORIENT, 2, QUART, 2 * QUART), bf16),
            pltpu.VMEM((here, IMG, QUART), bf16),
            pltpu.VMEM((here, QUART + 2 * REACH, QUART), bf16),
            pltpu.VMEM((frames, plane_window, QUART), bf16),
            pltpu.VMEM((planes, PLANE, here, ORIENT * 2, rows, QUART), bf16),
            pltpu.VMEM((frames, ORIENT, rows, 2 * QUART), bf16),
            pltpu.VMEM((ORIENT, frames, rows, QUART), bf16),
            pltpu.VMEM((total, total), bf16),
            pltpu.VMEM((frames // 2, rows, QUART), f32),
            pltpu.VMEM((frames, rows, QUART), f32),
            pltpu.VMEM((frames, rows, QUART), bf16),
            dma((3 + here * chunks,)),
            dma,
            dma((planes, here)),
            dma((planes, here)),
            dma((planes, here)),
            dma((planes, here)),
            dma((2 * planes, here)),
            dma((2 * planes, here)),
            dma((parts,)),
            dma((parts,)),
        ],
        compiler_params=pltpu.CompilerParams(
            collective_id=0, has_side_effects=True, vmem_limit_bytes=60 * 1024 * 1024
        ),
    )


def kernel_body(parts, video_frames, segments, ref_pick, band_taps):
    here = video_frames.shape[0]
    rows = QUART // parts
    down = down_table()
    return make_kernel(parts, here, rows)(
        segments,
        ref_pick,
        band_taps[None, :],
        video_frames,
        jnp.asarray(down),
        jnp.asarray(np.ascontiguousarray(down.T)),
        jnp.asarray(left_window(rows)),
        jnp.asarray(right_tables()),
    ).astype(jnp.float32)


def solution(mesh):
    parts = mesh.shape["frames"]
    if QUART % parts == 0 and (QUART // parts) % 16 == 0 and parts in (4, 8, 16):
        chosen = lambda *args: kernel_body(parts, *args)
    else:
        chosen = body
    in_specs = (P(("groups", "frames"), None, None), P("groups"), P("groups"), P())
    out_specs = P(("groups", "frames"), None, None)
    return jax.shard_map(chosen, mesh=mesh, in_specs=in_specs, out_specs=out_specs, check_vma=False)
```

profile of v0, /device:TPU:0, one launch (start us, length us, event | category | flops | bytes accessed | tf_op | source)
XLA Modules:
  0.0 37.2 jit_solution(10295035612098889874)
XLA Ops:
  0.0 35.4 %shard_map.82 = bf16[2,256,256]{2,1,0:T(8,128)(2,1)} custom-call(s32[32]{0:T(128)} %segments.1, s32[4]{0:T(128)} %picks.1, bf16[1,32]{1,0:T(2,128)(2,1)} %bitcast.1, bf16[2,1024,1024]{2,1,0:T(8,128)(2,1)} %video_hbm.1, bf16[256,1024]{1,0:T(8,128)(2,1)} %constant.8.clone.down_hbm, bf16[1024,256]{1,0:T(8,128)(2,1)} %constant.9.clone.down_t_hbm, ...), custom_call_target="tpu_custom_call" | custom-call | tf_op jit(solution)/shard_map/pallas_call | solution.py:571
  35.4 1.8 %convert_element_type.3 = f32[2,256,256]{2,1,0:T(8,128)} convert(bf16[2,256,256]{2,1,0:T(8,128)(2,1)} %shard_map.82) | non-fusion elementwise | flops 131072 | bytes 786432 | tf_op jit(solution)/shard_map/convert_element_type | solution.py:580
where the time goes:
time: 37.4 us; the launch traced here: 37.2 us
  Pallas kernels  35.4 us (95%)
  other arithmetic  1.78 us (5%)
    pallas_call x1, Pallas kernels, kernel_body(): make_kernel(parts, here, rows)  35.4 us
    convert_element_type x1, other arithmetic, kernel_body(): return make_kernel(parts, here, rows)(segments, ref_pick, band_taps[None,...  1.78 us

commit v1 on v0

--- a/solution.py
+++ b/solution.py
@@ -178,6 +178,7 @@
 
 PLANE = 4
 PAIR = 2
+LAG = 3
 
 
 def flip(number, bits):
@@ -194,19 +195,19 @@
     planes = parts // PLANE
     window = rows + 2 * REACH
     pair_window = PAIR * rows + 2 * REACH
-    plane_window = PLANE * rows + 2 * REACH
     total = frames * rows
     chunks = 2
 
     def kernel(
         segments, picks, taps, video_hbm, down_hbm, down_t_hbm, left, right_hbm, out_hbm,
-        video, down, down_t, right, half, reduced, gathered, stacked, coeffs,
+        video, down, down_t, right, half, column, beside, twin, stacked, coeffs,
         phase, matrix, numer, denom, moved,
-        load_sem, store_sem, send_1, recv_1, send_2, recv_2, send_3, recv_3, send_b, recv_b,
+        load_sem, store_sem, send_z, recv_z, send_x, recv_x, send_c, recv_c, send_b, recv_b,
     ):
         me = lax.axis_index("frames")
         plane, spot = me // PLANE, me % PLANE
         across, sibling = flip(spot, PAIR), flip(spot, 1)
+        side, core = spot // PAIR, spot % PAIR
         barrier = pltpu.get_barrier_semaphore()
 
         def peer(j):
@@ -230,90 +231,82 @@
                 load_down.start()
         load_right.start()
 
-        blank = jnp.zeros((frames, REACH, QUART), jnp.bfloat16)
-
-        @pl.when(plane == 0)
+        below, above = plane > 0, plane < planes - 1
+
+        def greet(where):
+            pl.semaphore_signal(barrier, inc=1, device_id={"frames": where})
+
+        greet(plane * PLANE + sibling)
+        greet(plane * PLANE + across)
+
+        @pl.when(below)
         def _():
-            gathered[:, :REACH, :] = blank
-
-        @pl.when(plane == planes - 1)
+            greet(me - PLANE)
+
+        @pl.when(above)
         def _():
-            gathered[:, plane_window - REACH :, :] = blank
-
-        @pl.loop(1, parts)
-        def _(j):
-            pl.semaphore_signal(barrier, inc=1, device_id={"frames": peer(j)})
-
-        edge = jnp.zeros((here, REACH, QUART), jnp.bfloat16)
-        reduced[:, :REACH, :] = edge
-        reduced[:, REACH + QUART :, :] = edge
-
-        def frame_of(j, where, n):
-            return (flip(plane, j) * PLANE + where) * here + n
-
-        def rows_of(j, n, first, size):
-            if j == 0:
-                start = pl.multiple_of((plane * PLANE + first) * rows, rows)
-                return reduced.at[n, pl.ds(start, size), :]
-            return gathered.at[frame_of(j, spot, n), pl.ds(pl.multiple_of(first * rows, rows), size), :]
-
-        def copy_1(j, n, low, high):
-            to = flip(plane, j)
-            start = pl.multiple_of(to * PLANE * rows + low, rows)
-            return pltpu.make_async_remote_copy(
-                src_ref=reduced.at[n, pl.ds(start, high - low), :],
-                dst_ref=gathered.at[me * here + n, pl.ds(low, high - low), :],
-                send_sem=send_1.at[j, n],
-                recv_sem=recv_1.at[j, n],
-                device_id={"frames": to * PLANE + spot},
-            )
-
-        def each_1(j, n, to, act):
-            @pl.when(to == 0)
-            def _():
-                act(copy_1(j, n, REACH, plane_window))
-
-            @pl.when(to == planes - 1)
-            def _():
-                act(copy_1(j, n, 0, plane_window - REACH))
-
-            if planes > 2:
-
-                @pl.when((to > 0) & (to < planes - 1))
-                def _():
-                    act(copy_1(j, n, 0, plane_window))
-
-        def copy_2(j, n):
-            first = across // PAIR * PAIR
-            where = pl.ds(pl.multiple_of(first * rows, rows), pair_window)
-            return pltpu.make_async_remote_copy(
-                src_ref=rows_of(j, n, first, pair_window),
-                dst_ref=gathered.at[frame_of(j, spot, n), where, :],
-                send_sem=send_2.at[j, n],
-                recv_sem=recv_2.at[j, n],
-                device_id={"frames": plane * PLANE + across},
-            )
-
-        sibling_rows = pl.ds(pl.multiple_of(sibling * rows, rows), window)
-
-        def copy_3(j, n):
-            return pltpu.make_async_remote_copy(
-                src_ref=rows_of(j, n, sibling, window),
-                dst_ref=gathered.at[frame_of(j, spot, n), sibling_rows, :],
-                send_sem=send_3.at[j, n],
-                recv_sem=recv_3.at[j, n],
-                device_id={"frames": plane * PLANE + sibling},
-            )
-
-        def copy_4(j, n):
-            part = gathered.at[frame_of(j, across, n), sibling_rows, :]
+            greet(me + PLANE)
+
+        blank = jnp.zeros((planes * here, REACH, QUART), jnp.bfloat16)
+        column[:, :REACH, :] = blank
+        column[:, REACH + QUART :, :] = blank
+
+        block = PLANE * rows
+        low, high = REACH, REACH + QUART
+
+        def z_copy(up, f, n, q):
+            first, last = (block * (q + 1), high) if up else (low, block * q + 2 * REACH)
+            part = column.at[f * here + n, first:last, :]
+            way = 0 if up else 1
             return pltpu.make_async_remote_copy(
                 src_ref=part,
                 dst_ref=part,
-                send_sem=send_3.at[planes + j, n],
-                recv_sem=recv_3.at[planes + j, n],
+                send_sem=send_z.at[way, f, n],
+                recv_sem=recv_z.at[way, f, n],
+                device_id={"frames": me + (PLANE if up else -PLANE)},
+            )
+
+        def z_each(up, f, n, act, receive=False):
+            for q in range(planes - 1) if up else range(1, planes):
+                here_if = q if not receive else (q + 1 if up else q - 1)
+
+                @pl.when(plane == here_if)
+                def _():
+                    act(z_copy(up, f, n, q))
+
+        def x_copy(f, n):
+            first = pl.multiple_of(plane * block + (1 - side) * PAIR * rows, rows)
+            return pltpu.make_async_remote_copy(
+                src_ref=column.at[f * here + n, pl.ds(first, pair_window), :],
+                dst_ref=beside.at[f * here + n],
+                send_sem=send_x.at[f, n],
+                recv_sem=recv_x.at[f, n],
+                device_id={"frames": plane * PLANE + across},
+            )
+
+        def core_copy(f, n):
+            first = pl.multiple_of(plane * block + sibling * rows, rows)
+            return pltpu.make_async_remote_copy(
+                src_ref=column.at[f * here + n, pl.ds(first, window), :],
+                dst_ref=twin.at[0, f * here + n],
+                send_sem=send_c.at[0, f, n],
+                recv_sem=recv_c.at[0, f, n],
                 device_id={"frames": plane * PLANE + sibling},
             )
+
+        def pass_copy(f, n):
+            first = pl.multiple_of((1 - core) * rows, rows)
+            return pltpu.make_async_remote_copy(
+                src_ref=beside.at[f * here + n, pl.ds(first, window), :],
+                dst_ref=twin.at[1, f * here + n],
+                send_sem=send_c.at[1, f, n],
+                recv_sem=recv_c.at[1, f, n],
+                device_id={"frames": plane * PLANE + sibling},
+            )
+
+        def spread_sideways(f, n):
+            x_copy(f, n).start()
+            core_copy(f, n).start()
 
         load_down_t.wait()
         for n in range(here):
@@ -325,15 +318,16 @@
                 ).astype(jnp.bfloat16)
             if n == 0:
                 load_down.wait()
-            reduced[n, REACH : REACH + QUART, :] = jnp.dot(
+            column[plane * here + n, REACH : REACH + QUART, :] = jnp.dot(
                 down[...], half[n], preferred_element_type=jnp.float32
             ).astype(jnp.bfloat16)
             if n == 0:
-                pl.semaphore_wait(barrier, parts - 1)
-            for j in range(1, planes):
-                each_1(j, n, flip(plane, j), lambda copy: copy.start())
-            copy_2(0, n).start()
-            copy_3(0, n).start()
+                pl.semaphore_wait(
+                    barrier, 2 + jnp.where(below, 1, 0) + jnp.where(above, 1, 0)
+                )
+            z_each(True, plane, n, lambda copy: copy.start())
+            z_each(False, plane, n, lambda copy: copy.start())
+            spread_sideways(plane, n)
 
         lag = lax.broadcasted_iota(jnp.int32, (frames, frames), 0) - lax.broadcasted_iota(
             jnp.int32, (frames, frames), 1
@@ -380,45 +374,81 @@
                 for p in range(planes):
                     coeffs[pl.ds((p * PLANE + where) * here, here), o] = value[p]
 
-        own_rows = pl.ds(pl.multiple_of(spot * rows, rows), window)
-
-        def stack_arrived(j, where):
-            @pl.loop(0, here)
-            def _(n):
-                t = frame_of(j, where, n)
-                stack_one((flip(plane, j), where, n), gathered[t, own_rows, :])
-
-        def second(j):
-            for n in range(here):
-                copy_2(j, n).wait_recv()
-                copy_4(j, n).start()
-            stack_arrived(j, across)
-
-        for n in range(here):
-            stack_one((plane, spot, n), reduced[n, pl.ds(pl.multiple_of(me * rows, rows), window), :])
-        for n in range(here):
-            for j in range(1, planes):
-                each_1(j, n, plane, lambda copy: copy.wait_recv())
-                copy_2(j, n).start()
-                copy_3(j, n).start()
-        for j in range(1, planes):
-            stack_arrived(j, spot)
+        own_rows = pl.ds(pl.multiple_of(plane * block + spot * rows, rows), window)
+        core_rows = pl.ds(pl.multiple_of(core * rows, rows), window)
+
+        def each(k, way, act):
+            if k == 0:
+                act(plane)
+            elif way == 0:
+
+                @pl.when(plane >= k)
+                def _():
+                    act(plane - k)
+
+            else:
+
+                @pl.when(plane + k < planes)
+                def _():
+                    act(plane + k)
+
+        def arrive(k, n, way):
+            def act(f):
+                z_each(way == 0, f, n, lambda copy: copy.wait_recv(), True)
+                z_each(way == 0, f, n, lambda copy: copy.start())
+                spread_sideways(f, n)
+
+            each(k, way, act)
+
+        def stack_column(k, n, way):
+            each(k, way, lambda f: stack_one((f, spot, n), column[f * here + n, own_rows, :]))
+
+        def stack_sibling(k, n, way):
+            def act(f):
+                core_copy(f, n).wait_recv()
+                stack_one((f, sibling, n), twin[0, f * here + n])
+
+            each(k, way, act)
+
+        def stack_across(k, n, way):
+            def act(f):
+                x_copy(f, n).wait_recv()
+                pass_copy(f, n).start()
+                stack_one((f, across, n), beside[f * here + n, core_rows, :])
+
+            each(k, way, act)
+
+        def stack_last(k, n, way):
+            def act(f):
+                pass_copy(f, n).wait_recv()
+                stack_one((f, flip(across, 1), n), twin[1, f * here + n])
+
+            each(k, way, act)
+
+        events = [(0, n, 0) for n in range(here)] + [
+            (k, n, way) for k in range(1, planes) for n in range(here) for way in range(2)
+        ]
+        late = LAG
+        for i, event in enumerate(events):
+            if event[0]:
+                arrive(*event)
+            stack_column(*event)
+            if i >= 1:
+                stack_sibling(*events[i - 1])
+            if i >= late:
+                stack_across(*events[i - late])
+            if i >= late + 1:
+                stack_last(*events[i - late - 1])
+        stack_sibling(*events[-1])
         load_right.wait()
-        for j in range(planes):
-            second(j)
         coefficients(spot)
-        for j in range(planes):
-            for n in range(here):
-                copy_3(j, n).wait_recv()
-            stack_arrived(j, sibling)
+        coefficients(sibling)
+        for event in events[len(events) - late :]:
+            stack_across(*event)
         coefficients(across)
-        coefficients(sibling)
-        last = flip(across, 1)
-        for j in range(planes):
-            for n in range(here):
-                copy_4(j, n).wait_recv()
-            stack_arrived(j, last)
-        coefficients(last)
+        for event in events[len(events) - late - 1 :]:
+            stack_last(*event)
+        coefficients(flip(across, 1))
 
         counts = [jnp.int32(0)] * NSEG
         for t in range(frames):
@@ -505,13 +535,18 @@
         )
         store.start()
 
-        for n in range(here):
-            for j in range(planes):
-                if j:
-                    each_1(j, n, flip(plane, j), lambda copy: copy.wait_send())
-                copy_2(j, n).wait_send()
-                copy_3(j, n).wait_send()
-                copy_4(j, n).wait_send()
+        for k, n, way in events:
+
+            def sent(f):
+                if k == 0 or way == 0:
+                    z_each(True, f, n, lambda copy: copy.wait_send())
+                if k == 0 or way == 1:
+                    z_each(False, f, n, lambda copy: copy.wait_send())
+                x_copy(f, n).wait_send()
+                core_copy(f, n).wait_send()
+                pass_copy(f, n).wait_send()
+
+            each(k, way, sent)
 
         @pl.loop(1, parts)
         def _(j):
@@ -538,8 +573,9 @@
             pltpu.VMEM((IMG, QUART), bf16),
             pltpu.VMEM((ORIENT, 2, QUART, 2 * QUART), bf16),
             pltpu.VMEM((here, IMG, QUART), bf16),
-            pltpu.VMEM((here, QUART + 2 * REACH, QUART), bf16),
-            pltpu.VMEM((frames, plane_window, QUART), bf16),
+            pltpu.VMEM((planes * here, QUART + 2 * REACH, QUART), bf16),
+            pltpu.VMEM((planes * here, pair_window, QUART), bf16),
+            pltpu.VMEM((2, planes * here, window, QUART), bf16),
             pltpu.VMEM((planes, PLANE, here, ORIENT * 2, rows, QUART), bf16),
             pltpu.VMEM((frames, ORIENT, rows, 2 * QUART), bf16),
             pltpu.VMEM((ORIENT, frames, rows, QUART), bf16),
@@ -549,12 +585,12 @@
             pltpu.VMEM((frames, rows, QUART), bf16),
             dma((3 + here * chunks,)),
             dma,
+            dma((2, planes, here)),
+            dma((2, planes, here)),
             dma((planes, here)),
             dma((planes, here)),
-            dma((planes, here)),
-            dma((planes, here)),
-            dma((2 * planes, here)),
-            dma((2 * planes, here)),
+            dma((2, planes, here)),
+            dma((2, planes, here)),
             dma((parts,)),
             dma((parts,)),
         ],

time: 37.4 us -> 36.6 us (0.979)
  Pallas kernels: 35.4 us -> 34.6 us
    pallas_call x1, Pallas kernels: 35.4 us -> 34.6 us  [kernel_body(): make_kernel(parts, here, rows)]
where the time goes in v1:
time: 36.6 us; the launch traced here: 36.3 us
  Pallas kernels  34.6 us (95%)
  other arithmetic  1.78 us (5%)
    pallas_call x1, Pallas kernels, kernel_body(): make_kernel(parts, here, rows)  34.6 us
    convert_element_type x1, other arithmetic, kernel_body(): return make_kernel(parts, here, rows)(segments, ref_pick, band_taps[None,...  1.78 us

profile of v1, /device:TPU:0, one launch (start us, length us, event | category | flops | bytes accessed | tf_op | source)
XLA Modules:
  0.0 36.3 jit_solution(14077331486887761885)
XLA Ops:
  0.0 34.6 %shard_map.82 = bf16[2,256,256]{2,1,0:T(8,128)(2,1)} custom-call(s32[32]{0:T(128)} %segments.1, s32[4]{0:T(128)} %picks.1, bf16[1,32]{1,0:T(2,128)(2,1)} %bitcast.1, bf16[2,1024,1024]{2,1,0:T(8,128)(2,1)} %video_hbm.1, bf16[256,1024]{1,0:T(8,128)(2,1)} %constant.8.clone.down_hbm, bf16[1024,256]{1,0:T(8,128)(2,1)} %constant.9.clone.down_t_hbm, ...), custom_call_target="tpu_custom_call" | custom-call | tf_op jit(solution)/shard_map/pallas_call | solution.py:607
  34.6 1.8 %convert_element_type.3 = f32[2,256,256]{2,1,0:T(8,128)} convert(bf16[2,256,256]{2,1,0:T(8,128)(2,1)} %shard_map.82) | non-fusion elementwise | flops 131072 | bytes 786432 | tf_op jit(solution)/shard_map/convert_element_type | solution.py:616

commit v2 on v1

--- a/solution.py
+++ b/solution.py
@@ -171,14 +171,15 @@
     envelope = gabor_envelope(offset)
     phase = waves()[0][:, None, None] * offset[None]
     real, imag = envelope * np.cos(phase), envelope * np.sin(phase)
-    upper = np.concatenate([real, imag], axis=2)
-    lower = np.concatenate([-imag, real], axis=2)
-    return np.stack([upper, lower], axis=1).astype(jnp.bfloat16)
+    return np.stack([real, imag], axis=1).astype(jnp.bfloat16)
 
 
 PLANE = 4
 PAIR = 2
 LAG = 3
+STRIP = 128
+UNROLL = 2
+ORDERS = ((0, 1, 2), (0, 1, 2))
 
 
 def flip(number, bits):
@@ -197,11 +198,12 @@
     pair_window = PAIR * rows + 2 * REACH
     total = frames * rows
     chunks = 2
+    strips = QUART // STRIP
 
     def kernel(
-        segments, picks, taps, video_hbm, down_hbm, down_t_hbm, left, right_hbm, out_hbm,
-        video, down, down_t, right, half, column, beside, twin, stacked, coeffs,
-        phase, matrix, numer, denom, moved,
+        segments, picks, taps, video_hbm, down_hbm, left, right_hbm, out_hbm,
+        video, down, right, half, column, beside, twin, stacked, coeffs,
+        powers, phase, matrix, denom, moved,
         load_sem, store_sem, send_z, recv_z, send_x, recv_x, send_c, recv_c, send_b, recv_b,
     ):
         me = lax.axis_index("frames")
@@ -220,32 +222,22 @@
                 video_hbm.at[n, where], video.at[n, where], load_sem.at[3 + n * chunks + part]
             )
 
-        load_down_t = pltpu.make_async_copy(down_t_hbm, down_t, load_sem.at[0])
         load_down = pltpu.make_async_copy(down_hbm, down, load_sem.at[1])
         load_right = pltpu.make_async_copy(right_hbm, right, load_sem.at[2])
-        load_down_t.start()
+        load_down.start()
         for n in range(here):
             for part in range(chunks):
                 piece(n, part).start()
-            if n == 0:
-                load_down.start()
         load_right.start()
-
-        below, above = plane > 0, plane < planes - 1
 
         def greet(where):
             pl.semaphore_signal(barrier, inc=1, device_id={"frames": where})
 
+        others = [flip(plane, j) for j in range(1, planes)]
+        for to in reversed(others):
+            greet(to * PLANE + spot)
+        greet(plane * PLANE + across)
         greet(plane * PLANE + sibling)
-        greet(plane * PLANE + across)
-
-        @pl.when(below)
-        def _():
-            greet(me - PLANE)
-
-        @pl.when(above)
-        def _():
-            greet(me + PLANE)
 
         blank = jnp.zeros((planes * here, REACH, QUART), jnp.bfloat16)
         column[:, :REACH, :] = blank
@@ -254,25 +246,25 @@
         block = PLANE * rows
         low, high = REACH, REACH + QUART
 
-        def z_copy(up, f, n, q):
-            first, last = (block * (q + 1), high) if up else (low, block * q + 2 * REACH)
-            part = column.at[f * here + n, first:last, :]
-            way = 0 if up else 1
+        def z_copy(f, n, q):
+            part = column.at[f * here + n, max(block * q, low) : min(block * (q + 2), high), :]
             return pltpu.make_async_remote_copy(
                 src_ref=part,
                 dst_ref=part,
-                send_sem=send_z.at[way, f, n],
-                recv_sem=recv_z.at[way, f, n],
-                device_id={"frames": me + (PLANE if up else -PLANE)},
-            )
-
-        def z_each(up, f, n, act, receive=False):
-            for q in range(planes - 1) if up else range(1, planes):
-                here_if = q if not receive else (q + 1 if up else q - 1)
-
-                @pl.when(plane == here_if)
+                send_sem=send_z.at[q, n],
+                recv_sem=recv_z.at[f, n],
+                device_id={"frames": q * PLANE + spot},
+            )
+
+        def z_part(f, n, to, act):
+            for q in range(planes):
+
+                @pl.when(to == q)
                 def _():
-                    act(z_copy(up, f, n, q))
+                    act(z_copy(f, n, q))
+
+        def z_send(n, to):
+            z_part(plane, n, to, lambda copy: copy.start())
 
         def x_copy(f, n):
             first = pl.multiple_of(plane * block + (1 - side) * PAIR * rows, rows)
@@ -308,26 +300,24 @@
             x_copy(f, n).start()
             core_copy(f, n).start()
 
-        load_down_t.wait()
+        load_down.wait()
         for n in range(here):
             for part in range(chunks):
                 piece(n, part).wait()
                 where = slice(part * (IMG // chunks), (part + 1) * (IMG // chunks))
-                half[n, where] = jnp.dot(
-                    video[n, where], down_t[...], preferred_element_type=jnp.float32
+                half[n, where] = lax.dot_general(
+                    video[n, where], down[...], (((1,), (1,)), ((), ())),
+                    preferred_element_type=jnp.float32,
                 ).astype(jnp.bfloat16)
-            if n == 0:
-                load_down.wait()
             column[plane * here + n, REACH : REACH + QUART, :] = jnp.dot(
                 down[...], half[n], preferred_element_type=jnp.float32
             ).astype(jnp.bfloat16)
             if n == 0:
-                pl.semaphore_wait(
-                    barrier, 2 + jnp.where(below, 1, 0) + jnp.where(above, 1, 0)
-                )
-            z_each(True, plane, n, lambda copy: copy.start())
-            z_each(False, plane, n, lambda copy: copy.start())
+                pl.semaphore_wait(barrier, planes + 1)
             spread_sideways(plane, n)
+            for i in ORDERS[min(n, 1)]:
+                if i < planes - 1:
+                    z_send(n, others[i])
 
         lag = lax.broadcasted_iota(jnp.int32, (frames, frames), 0) - lax.broadcasted_iota(
             jnp.int32, (frames, frames), 1
@@ -360,77 +350,70 @@
             )
 
         def coefficients(where):
+            tall_rows = planes * here * rows
+            total_power = [0.0] * strips
             for o in range(ORIENT):
-                value = jnp.dot(
-                    stacked[:, where, :, 2 * o].reshape(planes * here * rows, QUART),
-                    right[o, 0],
-                    preferred_element_type=jnp.float32,
-                ) + jnp.dot(
-                    stacked[:, where, :, 2 * o + 1].reshape(planes * here * rows, QUART),
-                    right[o, 1],
-                    preferred_element_type=jnp.float32,
-                )
-                value = value.astype(jnp.bfloat16).reshape(planes, here, rows, 2 * QUART)
+                even = stacked[:, where, :, 2 * o].reshape(tall_rows, QUART)
+                odd = stacked[:, where, :, 2 * o + 1].reshape(tall_rows, QUART)
+
+                def times(left_part, which):
+                    return jnp.dot(left_part, right[o, which], preferred_element_type=jnp.float32)
+
+                real = (times(even, 0) - times(odd, 1)).astype(jnp.bfloat16)
+                imag = (times(even, 1) + times(odd, 0)).astype(jnp.bfloat16)
+                wide_real, wide_imag = real.astype(jnp.float32), imag.astype(jnp.float32)
+                power = wide_real * wide_real + wide_imag * wide_imag
+                slot = slice(o % 2 * STRIP, (o % 2 + 1) * STRIP)
+                imag_slot = slice(QUART + o % 2 * STRIP, QUART + (o % 2 + 1) * STRIP)
+                for h in range(strips):
+                    columns = slice(h * STRIP, (h + 1) * STRIP)
+                    total_power[h] = total_power[h] + power[:, columns]
+
+                    def split(value):
+                        return value[:, columns].reshape(planes, here, rows, STRIP)
+
+                    for p in range(planes):
+                        at = pl.ds((p * PLANE + where) * here, here)
+                        coeffs[h, at, o // 2, :, slot] = split(real)[p]
+                        coeffs[h, at, o // 2, :, imag_slot] = split(imag)[p]
+                        powers[h, at, o // 2, :, slot] = split(power)[p]
+            for h in range(strips):
+                whole = (total_power[h] + 1.0).reshape(planes, here, rows, STRIP)
                 for p in range(planes):
-                    coeffs[pl.ds((p * PLANE + where) * here, here), o] = value[p]
+                    denom[h, pl.ds((p * PLANE + where) * here, here)] = whole[p]
 
         own_rows = pl.ds(pl.multiple_of(plane * block + spot * rows, rows), window)
         core_rows = pl.ds(pl.multiple_of(core * rows, rows), window)
 
-        def each(k, way, act):
-            if k == 0:
-                act(plane)
-            elif way == 0:
-
-                @pl.when(plane >= k)
-                def _():
-                    act(plane - k)
-
-            else:
-
-                @pl.when(plane + k < planes)
-                def _():
-                    act(plane + k)
-
-        def arrive(k, n, way):
-            def act(f):
-                z_each(way == 0, f, n, lambda copy: copy.wait_recv(), True)
-                z_each(way == 0, f, n, lambda copy: copy.start())
-                spread_sideways(f, n)
-
-            each(k, way, act)
-
-        def stack_column(k, n, way):
-            each(k, way, lambda f: stack_one((f, spot, n), column[f * here + n, own_rows, :]))
-
-        def stack_sibling(k, n, way):
-            def act(f):
-                core_copy(f, n).wait_recv()
-                stack_one((f, sibling, n), twin[0, f * here + n])
-
-            each(k, way, act)
-
-        def stack_across(k, n, way):
-            def act(f):
-                x_copy(f, n).wait_recv()
-                pass_copy(f, n).start()
-                stack_one((f, across, n), beside[f * here + n, core_rows, :])
-
-            each(k, way, act)
-
-        def stack_last(k, n, way):
-            def act(f):
-                pass_copy(f, n).wait_recv()
-                stack_one((f, flip(across, 1), n), twin[1, f * here + n])
-
-            each(k, way, act)
-
-        events = [(0, n, 0) for n in range(here)] + [
-            (k, n, way) for k in range(1, planes) for n in range(here) for way in range(2)
+        def arrive(f, n):
+            z_part(f, n, plane, lambda copy: copy.wait_recv())
+            spread_sideways(f, n)
+
+        def stack_column(f, n):
+            stack_one((f, spot, n), column[f * here + n, own_rows, :])
+
+        def stack_sibling(f, n):
+            core_copy(f, n).wait_recv()
+            stack_one((f, sibling, n), twin[0, f * here + n])
+
+        def stack_across(f, n):
+            x_copy(f, n).wait_recv()
+            pass_copy(f, n).start()
+            stack_one((f, across, n), beside[f * here + n, core_rows, :])
+
+        def stack_last(f, n):
+            pass_copy(f, n).wait_recv()
+            stack_one((f, flip(across, 1), n), twin[1, f * here + n])
+
+        events = [(plane, n) for n in range(here)] + [
+            (others[i], n)
+            for n in range(here)
+            for i in ORDERS[min(n, 1)]
+            if i < planes - 1
         ]
         late = LAG
         for i, event in enumerate(events):
-            if event[0]:
+            if i >= here:
                 arrive(*event)
             stack_column(*event)
             if i >= 1:
@@ -443,10 +426,10 @@
         load_right.wait()
         coefficients(spot)
         coefficients(sibling)
-        for event in events[len(events) - late :]:
+        for event in events[max(len(events) - late, 0) :]:
             stack_across(*event)
         coefficients(across)
-        for event in events[len(events) - late - 1 :]:
+        for event in events[max(len(events) - late - 1, 0) :]:
             stack_last(*event)
         coefficients(flip(across, 1))
 
@@ -462,101 +445,95 @@
             picked.append(first + rest)
             first = first + counts[s]
 
-        @pl.loop(0, frames)
-        def _(t):
-            ref = picked[NSEG - 1]
-            for s in range(NSEG - 1):
-                ref = jnp.where(segments[t] == s, picked[s], ref)
-            ones = coeffs[t].astype(jnp.float32)
-            base = coeffs[ref].astype(jnp.float32)
-            real, imag = ones[..., :QUART], ones[..., QUART:]
-            ref_real, ref_imag = base[..., :QUART], base[..., QUART:]
-            prod_real = real * ref_real + imag * ref_imag
-            prod_imag = imag * ref_real - real * ref_imag
-            signal = prod_imag * lax.rsqrt(prod_real * prod_real + prod_imag * prod_imag + 1.0)
-            phase[:, t] = signal.astype(jnp.bfloat16)
-            denom[t] = jnp.sum(real * real + imag * imag, axis=0) + 1.0
-
         here_rows = pl.ds(pl.multiple_of(me * rows, rows), rows)
 
-        def return_copy(j):
+        def phases(h):
+            @pl.loop(0, frames // UNROLL)
+            def _(step):
+                for u in range(UNROLL):
+                    t = step * UNROLL + u
+                    ref = picked[NSEG - 1]
+                    for s in range(NSEG - 1):
+                        ref = jnp.where(segments[t] == s, picked[s], ref)
+                    ones = coeffs[h, t].astype(jnp.float32)
+                    base = coeffs[h, ref].astype(jnp.float32)
+                    prod_imag = ones[..., QUART:] * base[..., :QUART] - ones[..., :QUART] * base[..., QUART:]
+                    signal = prod_imag * lax.rsqrt(powers[h, t] * powers[h, ref] + 1.0)
+                    phase[:, t] = signal.astype(jnp.bfloat16)
+
+        def return_copy(h, j):
             to = peer(j)
             return pltpu.make_async_remote_copy(
-                src_ref=moved.at[pl.ds(to * here, here)],
-                dst_ref=out_hbm.at[:, here_rows, :],
-                send_sem=send_b.at[j],
-                recv_sem=recv_b.at[j],
+                src_ref=moved.at[h, pl.ds(to * here, here)],
+                dst_ref=out_hbm.at[:, here_rows, h * STRIP : (h + 1) * STRIP],
+                send_sem=send_b.at[h, j],
+                recv_sem=recv_b.at[h, j],
                 device_id={"frames": to},
+            )
+
+        def store(h):
+            return pltpu.make_async_copy(
+                moved.at[h, pl.ds(me * here, here)],
+                out_hbm.at[:, here_rows, h * STRIP : (h + 1) * STRIP],
+                store_sem.at[h],
             )
 
         crowd = parts // 2
         near = me // crowd
 
-        def filter_half(number):
-            span = pl.ds(number * (frames // 2), frames // 2)
-            long_span = pl.ds(pl.multiple_of(number * (total // 2), total // 2), total // 2)
-            for o in range(ORIENT):
+        def filter_half(h, number):
+            span = slice(number * (frames // 2), (number + 1) * (frames // 2))
+            until = (number + 1) * (total // 2)
+            numer = 0.0
+            for q in range(ORIENT // 2):
                 filtered = (
                     jnp.dot(
-                        matrix[long_span, :],
-                        phase[o].reshape(total, QUART),
+                        matrix[number * (total // 2) : until, :until],
+                        phase[q].reshape(total, QUART)[:until],
                         preferred_element_type=jnp.float32,
                     )
                     .astype(jnp.bfloat16)
                     .astype(jnp.float32)
                     .reshape(frames // 2, rows, QUART)
                 )
-                real = coeffs[span, o, :, :QUART].astype(jnp.float32)
-                imag = coeffs[span, o, :, QUART:].astype(jnp.float32)
-                term = (real * real + imag * imag) * filtered
-                if o == 0:
-                    numer[...] = term
-                elif o < ORIENT - 1:
-                    numer[...] += term
-                else:
-                    moved[span] = ((numer[...] + term) / denom[span]).astype(jnp.bfloat16)
-
-        filter_half(1 - near)
-
-        @pl.loop(0, crowd)
-        def _(k):
-            to = (1 - near) * crowd + lax.rem(me + k, crowd)
-            return_copy(lax.rem(to + parts - me, parts)).start()
-
-        filter_half(near)
-
-        @pl.loop(1, crowd)
-        def _(k):
-            to = near * crowd + lax.rem(me + k, crowd)
-            return_copy(lax.rem(to + parts - me, parts)).start()
-
-        store = pltpu.make_async_copy(
-            moved.at[pl.ds(me * here, here)], out_hbm.at[:, here_rows, :], store_sem
-        )
-        store.start()
-
-        for k, n, way in events:
-
-            def sent(f):
-                if k == 0 or way == 0:
-                    z_each(True, f, n, lambda copy: copy.wait_send())
-                if k == 0 or way == 1:
-                    z_each(False, f, n, lambda copy: copy.wait_send())
-                x_copy(f, n).wait_send()
-                core_copy(f, n).wait_send()
-                pass_copy(f, n).wait_send()
-
-            each(k, way, sent)
-
-        @pl.loop(1, parts)
-        def _(j):
-            return_copy(j).wait_recv()
-
-        @pl.loop(1, parts)
-        def _(j):
-            return_copy(j).wait_send()
-
-        store.wait()
+                numer = numer + powers[h, span, q] * filtered
+            numer = numer[..., :STRIP] + numer[..., STRIP:]
+            moved[h, span] = (numer / denom[h, span]).astype(jnp.bfloat16)
+
+        for h in range(strips):
+            phases(h)
+            for close in (False, True):
+                for number in range(2):
+
+                    @pl.when((near == number) == close)
+                    def _():
+                        filter_half(h, number)
+
+                base_to = (near if close else 1 - near) * crowd
+
+                @pl.loop(1 if close else 0, crowd)
+                def _(k):
+                    to = base_to + lax.rem(me + k, crowd)
+                    return_copy(h, lax.rem(to + parts - me, parts)).start()
+
+            store(h).start()
+
+        for f, n in events:
+            x_copy(f, n).wait_send()
+            core_copy(f, n).wait_send()
+            pass_copy(f, n).wait_send()
+        for n in range(here):
+            for to in others:
+                z_part(plane, n, to, lambda copy: copy.wait_send())
+
+        for h in range(strips):
+
+            @pl.loop(1, parts)
+            def _(j):
+                return_copy(h, j).wait_recv()
+                return_copy(h, j).wait_send()
+
+            store(h).wait()
 
     bf16, f32, dma = jnp.bfloat16, jnp.float32, pltpu.SemaphoreType.DMA
     anywhere = pl.BlockSpec(memory_space=pl.ANY)
@@ -565,34 +542,33 @@
     return pl.pallas_call(
         kernel,
         out_shape=jax.ShapeDtypeStruct((here, QUART, QUART), bf16),
-        in_specs=[smem, smem, vmem, anywhere, anywhere, anywhere, vmem, anywhere],
+        in_specs=[smem, smem, vmem, anywhere, anywhere, vmem, anywhere],
         out_specs=anywhere,
         scratch_shapes=[
             pltpu.VMEM((here, IMG, IMG), bf16),
             pltpu.VMEM((QUART, IMG), bf16),
-            pltpu.VMEM((IMG, QUART), bf16),
-            pltpu.VMEM((ORIENT, 2, QUART, 2 * QUART), bf16),
+            pltpu.VMEM((ORIENT, 2, QUART, QUART), bf16),
             pltpu.VMEM((here, IMG, QUART), bf16),
             pltpu.VMEM((planes * here, QUART + 2 * REACH, QUART), bf16),
             pltpu.VMEM((planes * here, pair_window, QUART), bf16),
             pltpu.VMEM((2, planes * here, window, QUART), bf16),
             pltpu.VMEM((planes, PLANE, here, ORIENT * 2, rows, QUART), bf16),
-            pltpu.VMEM((frames, ORIENT, rows, 2 * QUART), bf16),
-            pltpu.VMEM((ORIENT, frames, rows, QUART), bf16),
+            pltpu.VMEM((strips, frames, ORIENT // 2, rows, 2 * QUART), bf16),
+            pltpu.VMEM((strips, frames, ORIENT // 2, rows, QUART), f32),
+            pltpu.VMEM((ORIENT // 2, frames, rows, QUART), bf16),
             pltpu.VMEM((total, total), bf16),
-            pltpu.VMEM((frames // 2, rows, QUART), f32),
-            pltpu.VMEM((frames, rows, QUART), f32),
-            pltpu.VMEM((frames, rows, QUART), bf16),
+            pltpu.VMEM((strips, frames, rows, STRIP), f32),
+            pltpu.VMEM((strips, frames, rows, STRIP), bf16),
             dma((3 + here * chunks,)),
-            dma,
-            dma((2, planes, here)),
-            dma((2, planes, here)),
+            dma((strips,)),
+            dma((planes, here)),
+            dma((planes, here)),
             dma((planes, here)),
             dma((planes, here)),
             dma((2, planes, here)),
             dma((2, planes, here)),
-            dma((parts,)),
-            dma((parts,)),
+            dma((strips, parts)),
+            dma((strips, parts)),
         ],
         compiler_params=pltpu.CompilerParams(
             collective_id=0, has_side_effects=True, vmem_limit_bytes=60 * 1024 * 1024
@@ -610,7 +586,6 @@
         band_taps[None, :],
         video_frames,
         jnp.asarray(down),
-        jnp.asarray(np.ascontiguousarray(down.T)),
         jnp.asarray(left_window(rows)),
         jnp.asarray(right_tables()),
     ).astype(jnp.float32)

time: 36.6 us -> 35.8 us (0.978)
  Pallas kernels: 34.6 us -> 33.8 us
    pallas_call x1, Pallas kernels: 34.6 us -> 33.8 us  [kernel_body(): make_kernel(parts, here, rows)]
where the time goes in v2:
time: 35.8 us; the launch traced here: 35.6 us
  Pallas kernels  33.8 us (94%)
  other arithmetic  1.78 us (5%)
    pallas_call x1, Pallas kernels, kernel_body(): make_kernel(parts, here, rows)  33.8 us
    convert_element_type x1, other arithmetic, kernel_body(): return make_kernel(parts, here, rows)(segments, ref_pick, band_taps[None,...  1.78 us

profile of v2, /device:TPU:0, one launch (start us, length us, event | category | flops | bytes accessed | tf_op | source)
XLA Modules:
  0.0 35.6 jit_solution(2225336279210527630)
XLA Ops:
  0.0 33.8 %shard_map.73 = bf16[2,256,256]{2,1,0:T(8,128)(2,1)} custom-call(s32[32]{0:T(128)} %segments.1, s32[4]{0:T(128)} %picks.1, bf16[1,32]{1,0:T(2,128)(2,1)} %bitcast.1, bf16[2,1024,1024]{2,1,0:T(8,128)(2,1)} %video_hbm.1, bf16[256,1024]{1,0:T(8,128)(2,1)} %constant.6.clone.down_hbm, bf16[128,80]{1,0:T(8,128)(2,1)} %constant.7.clone.left, ...), custom_call_target="tpu_custom_call" | custom-call | tf_op jit(solution)/shard_map/pallas_call | solution.py:583
  33.8 1.8 %convert_element_type.3 = f32[2,256,256]{2,1,0:T(8,128)} convert(bf16[2,256,256]{2,1,0:T(8,128)(2,1)} %shard_map.73) | non-fusion elementwise | flops 131072 | bytes 786432 | tf_op jit(solution)/shard_map/convert_element_type | solution.py:591

commit v3 on v2

--- a/solution.py
+++ b/solution.py
@@ -176,9 +176,10 @@
 
 PLANE = 4
 PAIR = 2
-LAG = 3
+LAG = 4
+DUE = 3
 STRIP = 128
-UNROLL = 2
+UNROLL = 4
 ORDERS = ((0, 1, 2), (0, 1, 2))
 
 
@@ -201,10 +202,10 @@
     strips = QUART // STRIP
 
     def kernel(
-        segments, picks, taps, video_hbm, down_hbm, left, right_hbm, out_hbm,
-        video, down, right, half, column, beside, twin, stacked, coeffs,
+        segments, picks, taps, video_hbm, down_hbm, down_t_hbm, left, right_hbm, out_hbm,
+        video, down, down_t, right, half, column, beside, twin, stacked, coeffs,
         powers, phase, matrix, denom, moved,
-        load_sem, store_sem, send_z, recv_z, send_x, recv_x, send_c, recv_c, send_b, recv_b,
+        load_sem, store_sem, send_z, recv_z, send_l, recv_l, send_x, recv_x, send_c, recv_c, send_b, recv_b,
     ):
         me = lax.axis_index("frames")
         plane, spot = me // PLANE, me % PLANE
@@ -223,11 +224,14 @@
             )
 
         load_down = pltpu.make_async_copy(down_hbm, down, load_sem.at[1])
+        load_down_t = pltpu.make_async_copy(down_t_hbm, down_t, load_sem.at[0])
         load_right = pltpu.make_async_copy(right_hbm, right, load_sem.at[2])
-        load_down.start()
+        load_down_t.start()
         for n in range(here):
             for part in range(chunks):
                 piece(n, part).start()
+            if n == 0:
+                load_down.start()
         load_right.start()
 
         def greet(where):
@@ -246,8 +250,25 @@
         block = PLANE * rows
         low, high = REACH, REACH + QUART
 
+        def early(q):
+            return 0 if q < max(planes // 2, 1) else 1
+
+        ahead = side == jnp.where(plane < max(planes // 2, 1), 0, 1)
+
+        def bounds(first, last):
+            return max(first, low), min(last, high)
+
+        def early_rows(q):
+            first = block * q + (PAIR * rows if early(q) else 0)
+            return bounds(first, first + pair_window)
+
+        def late_rows(q):
+            first = block * q + (0 if early(q) else pair_window)
+            return bounds(first, first + PAIR * rows)
+
         def z_copy(f, n, q):
-            part = column.at[f * here + n, max(block * q, low) : min(block * (q + 2), high), :]
+            first, last = early_rows(q)
+            part = column.at[f * here + n, first:last, :]
             return pltpu.make_async_remote_copy(
                 src_ref=part,
                 dst_ref=part,
@@ -266,15 +287,72 @@
         def z_send(n, to):
             z_part(plane, n, to, lambda copy: copy.start())
 
-        def x_copy(f, n):
-            first = pl.multiple_of(plane * block + (1 - side) * PAIR * rows, rows)
+        def late_copy(f, n, q, straight):
+            first, last = late_rows(q)
+            inside = 0 if early(q) else pair_window - PAIR * rows
+            inside = inside + first - (block * q + (0 if early(q) else pair_window))
+            target = (
+                column.at[f * here + n, first:last, :]
+                if straight
+                else beside.at[f * here + n, inside : inside + last - first, :]
+            )
+            other_side = 1 - early(q)
             return pltpu.make_async_remote_copy(
-                src_ref=column.at[f * here + n, pl.ds(first, pair_window), :],
-                dst_ref=beside.at[f * here + n],
+                src_ref=column.at[f * here + n, first:last, :],
+                dst_ref=target,
+                send_sem=send_l.at[q, n],
+                recv_sem=recv_l.at[0 if straight else 1, f, n],
+                device_id={"frames": q * PLANE + other_side * PAIR + core},
+            )
+
+        def has_late(q):
+            first, last = late_rows(q)
+            return last > first
+
+        def late_own(n, act):
+            for q in range(planes):
+                if has_late(q):
+
+                    @pl.when((side == 1 - early(q)) & (plane != q))
+                    def _():
+                        act(late_copy(plane, n, q, True))
+
+                    @pl.when(side == early(q))
+                    def _():
+                        act(late_copy(plane, n, q, False))
+
+        def late_wait(f, n, straight):
+            for q in range(planes):
+                if has_late(q):
+
+                    @pl.when(plane == q)
+                    def _():
+                        late_copy(f, n, q, straight).wait_recv()
+
+        def x_copy(f, n, q, whole):
+            first = block * q + (PAIR * rows if early(q) else 0)
+            inside, size = 0, pair_window
+            if not whole:
+                first, size = block * q + PAIR * rows, pair_window - PAIR * rows
+                inside = PAIR * rows if early(q) else 0
+            return pltpu.make_async_remote_copy(
+                src_ref=column.at[f * here + n, first : first + size, :],
+                dst_ref=beside.at[f * here + n, inside : inside + size, :],
                 send_sem=send_x.at[f, n],
                 recv_sem=recv_x.at[f, n],
                 device_id={"frames": plane * PLANE + across},
             )
+
+        def x_each(f, n, to_ahead, act):
+            for q in range(planes):
+                for whole in (False, True):
+
+                    @pl.when((plane == q) & (to_ahead == whole))
+                    def _():
+                        act(x_copy(f, n, q, whole))
+
+        def x_send(f, n):
+            x_each(f, n, ~ahead, lambda copy: copy.start())
 
         def core_copy(f, n):
             first = pl.multiple_of(plane * block + sibling * rows, rows)
@@ -296,28 +374,38 @@
                 device_id={"frames": plane * PLANE + sibling},
             )
 
-        def spread_sideways(f, n):
-            x_copy(f, n).start()
-            core_copy(f, n).start()
-
-        load_down.wait()
+        load_down_t.wait()
         for n in range(here):
             for part in range(chunks):
                 piece(n, part).wait()
                 where = slice(part * (IMG // chunks), (part + 1) * (IMG // chunks))
-                half[n, where] = lax.dot_general(
-                    video[n, where], down[...], (((1,), (1,)), ((), ())),
-                    preferred_element_type=jnp.float32,
+                half[n, where] = jnp.dot(
+                    video[n, where], down_t[...], preferred_element_type=jnp.float32
                 ).astype(jnp.bfloat16)
+            if n == 0:
+                load_down.wait()
             column[plane * here + n, REACH : REACH + QUART, :] = jnp.dot(
                 down[...], half[n], preferred_element_type=jnp.float32
             ).astype(jnp.bfloat16)
             if n == 0:
                 pl.semaphore_wait(barrier, planes + 1)
-            spread_sideways(plane, n)
+            x_send(plane, n)
+            core_copy(plane, n).start()
             for i in ORDERS[min(n, 1)]:
                 if i < planes - 1:
                     z_send(n, others[i])
+
+        counts = [jnp.int32(0)] * NSEG
+        for t in range(frames):
+            for s in range(NSEG):
+                counts[s] = counts[s] + jnp.where(segments[t] == s, 1, 0)
+        picked, first = [], jnp.int32(0)
+        for s in range(NSEG):
+            rest = picks[s]
+            for bit in reversed(range((PICK_LIMIT - 1).bit_length())):
+                rest = jnp.where(rest >= counts[s] * (1 << bit), rest - counts[s] * (1 << bit), rest)
+            picked.append(first + rest)
+            first = first + counts[s]
 
         lag = lax.broadcasted_iota(jnp.int32, (frames, frames), 0) - lax.broadcasted_iota(
             jnp.int32, (frames, frames), 1
@@ -385,25 +473,32 @@
         own_rows = pl.ds(pl.multiple_of(plane * block + spot * rows, rows), window)
         core_rows = pl.ds(pl.multiple_of(core * rows, rows), window)
 
-        def arrive(f, n):
-            z_part(f, n, plane, lambda copy: copy.wait_recv())
-            spread_sideways(f, n)
-
         def stack_column(f, n):
             stack_one((f, spot, n), column[f * here + n, own_rows, :])
 
+        def stack_twin(f, n):
+            stack_one((f, sibling, n), twin[0, f * here + n])
+
         def stack_sibling(f, n):
             core_copy(f, n).wait_recv()
-            stack_one((f, sibling, n), twin[0, f * here + n])
+            stack_twin(f, n)
+
+        def x_wait(f, n):
+            x_each(f, n, ahead, lambda copy: copy.wait_recv())
+
+        def stack_beside(f, n):
+            stack_one((f, across, n), beside[f * here + n, core_rows, :])
+
+        def stack_passed(f, n):
+            stack_one((f, flip(across, 1), n), twin[1, f * here + n])
 
         def stack_across(f, n):
-            x_copy(f, n).wait_recv()
             pass_copy(f, n).start()
-            stack_one((f, across, n), beside[f * here + n, core_rows, :])
+            stack_beside(f, n)
 
         def stack_last(f, n):
             pass_copy(f, n).wait_recv()
-            stack_one((f, flip(across, 1), n), twin[1, f * here + n])
+            stack_passed(f, n)
 
         events = [(plane, n) for n in range(here)] + [
             (others[i], n)
@@ -411,39 +506,77 @@
             for i in ORDERS[min(n, 1)]
             if i < planes - 1
         ]
-        late = LAG
-        for i, event in enumerate(events):
+        held_back = len(events) - LAG
+        for i, (f, n) in enumerate(events):
             if i >= here:
-                arrive(*event)
-            stack_column(*event)
-            if i >= 1:
-                stack_sibling(*events[i - 1])
-            if i >= late:
-                stack_across(*events[i - late])
-            if i >= late + 1:
-                stack_last(*events[i - late - 1])
+                z_part(f, n, plane, lambda copy: copy.wait_recv())
+                x_send(f, n)
+
+                @pl.when(ahead)
+                def _():
+                    core_copy(f, n).start()
+
+            if i == min(LAG, DUE):
+                x_wait(*events[0])
+            if i == DUE:
+                for m in range(here):
+                    late_own(m, lambda copy: copy.start())
+
+            @pl.when(ahead)
+            def _():
+                stack_column(f, n)
+                if i >= 1:
+                    stack_sibling(*events[i - 1])
+                if i >= LAG:
+                    if i > LAG:
+                        x_wait(*events[i - LAG])
+                    stack_across(*events[i - LAG])
+                if i >= LAG + 1:
+                    stack_last(*events[i - LAG - 1])
+
+        @pl.when(~ahead)
+        def _():
+            for f, n in events[here:]:
+                late_wait(f, n, True)
+                core_copy(f, n).start()
+            for event in events:
+                stack_column(*event)
+            for f, n in events[:-1]:
+                core_copy(f, n).wait_recv()
+            for event in events[:-1]:
+                stack_twin(*event)
+            for i, (f, n) in enumerate(events[:held_back]):
+                if i:
+                    x_wait(f, n)
+                late_wait(f, n, False)
+                pass_copy(f, n).start()
+            for event in events[:held_back]:
+                stack_beside(*event)
+            for f, n in events[: held_back - 1]:
+                pass_copy(f, n).wait_recv()
+            for event in events[: held_back - 1]:
+                stack_passed(*event)
+
         stack_sibling(*events[-1])
         load_right.wait()
         coefficients(spot)
         coefficients(sibling)
-        for event in events[max(len(events) - late, 0) :]:
-            stack_across(*event)
+        for f, n in events[held_back:]:
+            x_wait(f, n)
+
+            @pl.when(~ahead)
+            def _():
+                late_wait(f, n, False)
+
+            pass_copy(f, n).start()
+        for event in events[held_back:]:
+            stack_beside(*event)
         coefficients(across)
-        for event in events[max(len(events) - late - 1, 0) :]:
-            stack_last(*event)
+        for f, n in events[held_back - 1 :]:
+            pass_copy(f, n).wait_recv()
+        for event in events[held_back - 1 :]:
+            stack_passed(*event)
         coefficients(flip(across, 1))
-
-        counts = [jnp.int32(0)] * NSEG
-        for t in range(frames):
-            for s in range(NSEG):
-                counts[s] = counts[s] + jnp.where(segments[t] == s, 1, 0)
-        picked, first = [], jnp.int32(0)
-        for s in range(NSEG):
-            rest = picks[s]
-            for bit in reversed(range((PICK_LIMIT - 1).bit_length())):
-                rest = jnp.where(rest >= counts[s] * (1 << bit), rest - counts[s] * (1 << bit), rest)
-            picked.append(first + rest)
-            first = first + counts[s]
 
         here_rows = pl.ds(pl.multiple_of(me * rows, rows), rows)
 
@@ -519,12 +652,13 @@
             store(h).start()
 
         for f, n in events:
-            x_copy(f, n).wait_send()
+            x_each(f, n, ~ahead, lambda copy: copy.wait_send())
             core_copy(f, n).wait_send()
             pass_copy(f, n).wait_send()
         for n in range(here):
             for to in others:
                 z_part(plane, n, to, lambda copy: copy.wait_send())
+            late_own(n, lambda copy: copy.wait_send())
 
         for h in range(strips):
 
@@ -542,11 +676,12 @@
     return pl.pallas_call(
         kernel,
         out_shape=jax.ShapeDtypeStruct((here, QUART, QUART), bf16),
-        in_specs=[smem, smem, vmem, anywhere, anywhere, vmem, anywhere],
+        in_specs=[smem, smem, vmem, anywhere, anywhere, anywhere, vmem, anywhere],
         out_specs=anywhere,
         scratch_shapes=[
             pltpu.VMEM((here, IMG, IMG), bf16),
             pltpu.VMEM((QUART, IMG), bf16),
+            pltpu.VMEM((IMG, QUART), bf16),
             pltpu.VMEM((ORIENT, 2, QUART, QUART), bf16),
             pltpu.VMEM((here, IMG, QUART), bf16),
             pltpu.VMEM((planes * here, QUART + 2 * REACH, QUART), bf16),
@@ -564,6 +699,8 @@
             dma((planes, here)),
             dma((planes, here)),
             dma((planes, here)),
+            dma((2, planes, here)),
+            dma((planes, here)),
             dma((planes, here)),
             dma((2, planes, here)),
             dma((2, planes, here)),
@@ -586,6 +723,7 @@
         band_taps[None, :],
         video_frames,
         jnp.asarray(down),
+        jnp.asarray(np.ascontiguousarray(down.T)),
         jnp.asarray(left_window(rows)),
         jnp.asarray(right_tables()),
     ).astype(jnp.float32)

time: 35.8 us -> 35 us (0.978)
  Pallas kernels: 33.8 us -> 33 us
    pallas_call x1, Pallas kernels: 33.8 us -> 33 us  [kernel_body(): make_kernel(parts, here, rows)]
where the time goes in v3:
time: 35 us; the launch traced here: 34.8 us
  Pallas kernels  33 us (94%)
  other arithmetic  1.78 us (5%)
    pallas_call x1, Pallas kernels, kernel_body(): make_kernel(parts, here, rows)  33 us
    convert_element_type x1, other arithmetic, kernel_body(): return make_kernel(parts, here, rows)(segments, ref_pick, band_taps[None,...  1.78 us

profile of v3, /device:TPU:0, one launch (start us, length us, event | category | flops | bytes accessed | tf_op | source)
XLA Modules:
  0.0 34.8 jit_solution(886149708878244371)
XLA Ops:
  0.0 33.0 %shard_map.82 = bf16[2,256,256]{2,1,0:T(8,128)(2,1)} custom-call(s32[32]{0:T(128)} %segments.1, s32[4]{0:T(128)} %picks.1, bf16[1,32]{1,0:T(2,128)(2,1)} %bitcast.1, bf16[2,1024,1024]{2,1,0:T(8,128)(2,1)} %video_hbm.1, bf16[256,1024]{1,0:T(8,128)(2,1)} %constant.8.clone.down_hbm, bf16[1024,256]{1,0:T(8,128)(2,1)} %constant.9.clone.down_t_hbm, ...), custom_call_target="tpu_custom_call" | custom-call | tf_op jit(solution)/shard_map/pallas_call | solution.py:720
  33.0 1.8 %convert_element_type.3 = f32[2,256,256]{2,1,0:T(8,128)} convert(bf16[2,256,256]{2,1,0:T(8,128)(2,1)} %shard_map.82) | non-fusion elementwise | flops 131072 | bytes 786432 | tf_op jit(solution)/shard_map/convert_element_type | solution.py:729

commit v4 on v3

--- a/solution.py
+++ b/solution.py
@@ -176,7 +176,7 @@
 
 PLANE = 4
 PAIR = 2
-LAG = 4
+LAG = 3
 DUE = 3
 STRIP = 128
 UNROLL = 4
@@ -536,26 +536,32 @@
 
         @pl.when(~ahead)
         def _():
-            for f, n in events[here:]:
-                late_wait(f, n, True)
-                core_copy(f, n).start()
-            for event in events:
-                stack_column(*event)
-            for f, n in events[:-1]:
-                core_copy(f, n).wait_recv()
-            for event in events[:-1]:
-                stack_twin(*event)
-            for i, (f, n) in enumerate(events[:held_back]):
-                if i:
-                    x_wait(f, n)
-                late_wait(f, n, False)
-                pass_copy(f, n).start()
-            for event in events[:held_back]:
-                stack_beside(*event)
-            for f, n in events[: held_back - 1]:
-                pass_copy(f, n).wait_recv()
-            for event in events[: held_back - 1]:
-                stack_passed(*event)
+            middle = here + planes - 1
+            for group in (range(middle), range(middle, len(events))):
+                forward = [i for i in group if i < held_back]
+                for i in group:
+                    if i >= here:
+                        late_wait(*events[i], True)
+                        core_copy(*events[i]).start()
+                for i in forward:
+                    if i:
+                        x_wait(*events[i])
+                    late_wait(*events[i], False)
+                    pass_copy(*events[i]).start()
+                for i in group:
+                    stack_column(*events[i])
+                for i in forward:
+                    stack_beside(*events[i])
+                twins = [i for i in group if i < len(events) - 1]
+                for i in twins:
+                    core_copy(*events[i]).wait_recv()
+                for i in twins:
+                    stack_twin(*events[i])
+                ready = [i for i in forward if i < held_back - 1]
+                for i in ready:
+                    pass_copy(*events[i]).wait_recv()
+                for i in ready:
+                    stack_passed(*events[i])
 
         stack_sibling(*events[-1])
         load_right.wait()

time: 35 us -> 34.4 us (0.983)
  Pallas kernels: 33 us -> 32.4 us
    pallas_call x1, Pallas kernels: 33 us -> 32.4 us  [kernel_body(): make_kernel(parts, here, rows)]
where the time goes in v4:
time: 34.4 us; the launch traced here: 34.2 us
  Pallas kernels  32.4 us (94%)
  other arithmetic  1.78 us (5%)
    pallas_call x1, Pallas kernels, kernel_body(): make_kernel(parts, here, rows)  32.4 us
    convert_element_type x1, other arithmetic, kernel_body(): return make_kernel(parts, here, rows)(segments, ref_pick, band_taps[None,...  1.78 us

profile of v4, /device:TPU:0, one launch (start us, length us, event | category | flops | bytes accessed | tf_op | source)
XLA Modules:
  0.0 34.2 jit_solution(10011665482669090872)
XLA Ops:
  0.0 32.4 %shard_map.82 = bf16[2,256,256]{2,1,0:T(8,128)(2,1)} custom-call(s32[32]{0:T(128)} %segments.1, s32[4]{0:T(128)} %picks.1, bf16[1,32]{1,0:T(2,128)(2,1)} %bitcast.1, bf16[2,1024,1024]{2,1,0:T(8,128)(2,1)} %video_hbm.1, bf16[256,1024]{1,0:T(8,128)(2,1)} %constant.8.clone.down_hbm, bf16[1024,256]{1,0:T(8,128)(2,1)} %constant.9.clone.down_t_hbm, ...), custom_call_target="tpu_custom_call" | custom-call | tf_op jit(solution)/shard_map/pallas_call | solution.py:726
  32.4 1.8 %convert_element_type.3 = f32[2,256,256]{2,1,0:T(8,128)} convert(bf16[2,256,256]{2,1,0:T(8,128)(2,1)} %shard_map.82) | non-fusion elementwise | flops 131072 | bytes 786432 | tf_op jit(solution)/shard_map/convert_element_type | solution.py:735

commit v5 on v4

--- a/solution.py
+++ b/solution.py
@@ -522,10 +522,16 @@
                 for m in range(here):
                     late_own(m, lambda copy: copy.start())
 
+            if i < here:
+                stack_column(f, n)
+            if 1 <= i <= here:
+                stack_sibling(*events[i - 1])
+
             @pl.when(ahead)
             def _():
-                stack_column(f, n)
-                if i >= 1:
+                if i >= here:
+                    stack_column(f, n)
+                if i > here:
                     stack_sibling(*events[i - 1])
                 if i >= LAG:
                     if i > LAG:
@@ -549,10 +555,11 @@
                     late_wait(*events[i], False)
                     pass_copy(*events[i]).start()
                 for i in group:
-                    stack_column(*events[i])
+                    if i >= here:
+                        stack_column(*events[i])
                 for i in forward:
                     stack_beside(*events[i])
-                twins = [i for i in group if i < len(events) - 1]
+                twins = [i for i in group if here <= i < len(events) - 1]
                 for i in twins:
                     core_copy(*events[i]).wait_recv()
                 for i in twins:

time: 34.4 us -> 34.4 us (level)
  no operation moved by 1% of the time
where the time goes in v5:
time: 34.4 us; the launch traced here: 34.2 us
  Pallas kernels  32.5 us (94%)
  other arithmetic  1.78 us (5%)
    pallas_call x1, Pallas kernels, kernel_body(): make_kernel(parts, here, rows)  32.5 us
    convert_element_type x1, other arithmetic, kernel_body(): return make_kernel(parts, here, rows)(segments, ref_pick, band_taps[None,...  1.78 us

profile of v5, /device:TPU:0, one launch (start us, length us, event | category | flops | bytes accessed | tf_op | source)
XLA Modules:
  0.0 34.2 jit_solution(4475947230994326445)
XLA Ops:
  0.0 32.5 %shard_map.82 = bf16[2,256,256]{2,1,0:T(8,128)(2,1)} custom-call(s32[32]{0:T(128)} %segments.1, s32[4]{0:T(128)} %picks.1, bf16[1,32]{1,0:T(2,128)(2,1)} %bitcast.1, bf16[2,1024,1024]{2,1,0:T(8,128)(2,1)} %video_hbm.1, bf16[256,1024]{1,0:T(8,128)(2,1)} %constant.8.clone.down_hbm, bf16[1024,256]{1,0:T(8,128)(2,1)} %constant.9.clone.down_t_hbm, ...), custom_call_target="tpu_custom_call" | custom-call | tf_op jit(solution)/shard_map/pallas_call | solution.py:733
  32.5 1.8 %convert_element_type.3 = f32[2,256,256]{2,1,0:T(8,128)} convert(bf16[2,256,256]{2,1,0:T(8,128)(2,1)} %shard_map.82) | non-fusion elementwise | flops 131072 | bytes 786432 | tf_op jit(solution)/shard_map/convert_element_type | solution.py:742
